TPU v7x, 512 devices: a whole 4x8x8 slice. The times are simulated.
512 devices in a mesh: dp: 64 (over z_lo, y, x), seq: 8 (over z_hi, core).
Axes of the slice: x: 4, y: 8, z: 8 (z_hi: 4, z_lo: 2; z = z_hi * 2 + z_lo), core: 2. Of those that a mesh axis runs over, the one named last changes fastest.
Arguments:
- queries: bfloat16 [65536, 4096], P(('dp', 'seq')), may hold values from -48 to 48
- keys: bfloat16 [65536, 1024], P(('dp', 'seq')), may hold values from -6 to 6
- values: bfloat16 [65536, 1024], P(('dp', 'seq')), may hold values from -6 to 6
- out_grad: bfloat16 [65536, 4096], P(('dp', 'seq')), may hold values from -6 to 6
- normed: bfloat16 [65536, 4096], P(('dp', 'seq')), may hold values from -24 to 24
Outputs:
- query_grad: bfloat16 [65536, 4096], P(('dp', 'seq'))
- key_weight_grad: float32 [4096, 1024], P('dp', 'seq')
- value_weight_grad: float32 [4096, 1024], P('dp', 'seq')
All inputs are finite; a program needn't handle non-finite values.
Results may differ from a plain program's by a relative error of at most 0.0055.
Values may be sent and summed in bfloat16 or wider, within the bound.
A program may use at most 128 MiB of HBM per device.

v0:
```python
import math
import jax
import jax.numpy as jnp
from jax import lax
from jax.sharding import PartitionSpec as P

HD = 128


def unrotate(grad, position):
    half = HD // 2
    freqs = jnp.exp(-math.log(500000.0) * (2.0 * jnp.arange(half).astype(jnp.float32) / HD))
    angle = position.astype(jnp.float32)[:, None] * freqs[None, :]
    cosine = jnp.cos(angle)[:, None, :]
    sine = jnp.sin(angle)[:, None, :]
    first = grad[..., :half]
    second = grad[..., half:]
    return jnp.concatenate(
        [first * cosine + second * sine, second * cosine - first * sine], axis=-1
    )


def local(queries, keys, values, out_grad, normed):
    head_q, head_k, head_v, head_g = (
        lax.all_to_all(queries, "seq", split_axis=1, concat_axis=0, tiled=True),
        lax.all_to_all(keys, "seq", split_axis=1, concat_axis=0, tiled=True),
        lax.all_to_all(values, "seq", split_axis=1, concat_axis=0, tiled=True),
        lax.all_to_all(out_grad, "seq", split_axis=1, concat_axis=0, tiled=True),
    )
    length = head_q.shape[0]
    heads = head_q.shape[1] // HD
    kv_heads = head_k.shape[1] // HD
    groups = heads // kv_heads
    scale = 1.0 / math.sqrt(HD)
    block = max(512, length // 8)
    starts = list(range(0, length, block))
    query_parts = [[None] * heads for first in starts]
    high = HD
    key_acc = jnp.zeros((length, HD), jnp.float32)
    value_acc = jnp.zeros((length, HD), jnp.float32)
    for number, first in enumerate(starts):
        last = first + block
        query_pos = first + jnp.arange(block)[:, None]
        key_pos = jnp.arange(last)[None, :]
        allowed = key_pos <= query_pos
        key_block = head_k[:last, 0:high]
        value_block = head_v[:last, 0:high]
        for member in range(groups):
            query_block = head_q[first:last, member * HD : (member + 1) * HD]
            grad_block = head_g[first:last, member * HD : (member + 1) * HD]
            scores = (
                lax.dot_general(
                    query_block,
                    key_block,
                    (((1,), (1,)), ((), ())),
                    preferred_element_type=jnp.float32,
                )
                * scale
            )
            scores = jnp.where(allowed, scores, -jnp.inf)
            top = jnp.max(scores, axis=1, keepdims=True)
            expo = jnp.where(allowed, jnp.exp(scores - top), 0.0)
            probs = expo / jnp.sum(expo, axis=1, keepdims=True)
            probs_b = probs.astype(jnp.bfloat16)
            value_acc = value_acc.at[:last].add(
                lax.dot_general(
                    probs_b,
                    grad_block,
                    (((0,), (0,)), ((), ())),
                    preferred_element_type=jnp.float32,
                )
            )
            prob_grad = lax.dot_general(
                grad_block,
                value_block,
                (((1,), (1,)), ((), ())),
                preferred_element_type=jnp.float32,
            )
            delta = jnp.sum(probs * prob_grad, axis=1, keepdims=True)
            score_grad = (probs * (prob_grad - delta) * scale).astype(jnp.bfloat16)
            query_parts[number][member] = jnp.dot(
                score_grad, key_block, preferred_element_type=jnp.float32
            ).astype(jnp.bfloat16)
            key_acc = key_acc.at[:last].add(
                lax.dot_general(
                    score_grad,
                    query_block,
                    (((0,), (0,)), ((), ())),
                    preferred_element_type=jnp.float32,
                )
            )
    key_groups = [key_acc]
    head_query_grad = jnp.concatenate(
        [jnp.concatenate(parts, axis=1) for parts in query_parts], axis=0
    )
    rows_pos = jnp.arange(length)
    key_total = jnp.stack(key_groups, axis=1)
    key_grad = unrotate(key_total, rows_pos).reshape(length, kv_heads * HD).astype(jnp.bfloat16)
    value_grad = value_acc.astype(jnp.bfloat16)
    query_grad = lax.all_to_all(head_query_grad, "seq", split_axis=0, concat_axis=1, tiled=True)
    width = normed.shape[1]
    piece = lax.all_gather(normed, "seq", axis=0, tiled=True)
    key_part = lax.dot_general(
        piece, key_grad, (((0,), (0,)), ((), ())), preferred_element_type=jnp.float32
    )
    value_part = lax.dot_general(
        piece, value_grad, (((0,), (0,)), ((), ())), preferred_element_type=jnp.float32
    )
    key_full, value_full = lax.psum((key_part, value_part), "dp")
    share = width // lax.axis_size("dp")
    offset = lax.axis_index("dp") * share
    key_weight_grad = lax.dynamic_slice_in_dim(key_full, offset, share, 0)
    value_weight_grad = lax.dynamic_slice_in_dim(value_full, offset, share, 0)
    return (query_grad, key_weight_grad, value_weight_grad)


def solution(mesh):
    placed = (
        P(("dp", "seq"), None),
        P(("dp", "seq"), None),
        P(("dp", "seq"), None),
        P(("dp", "seq"), None),
        P(("dp", "seq"), None),
    )
    return jax.shard_map(
        local,
        mesh=mesh,
        in_specs=placed,
        out_specs=(P(("dp", "seq"), None), P("dp", "seq"), P("dp", "seq")),
        check_vma=False,
    )
```

profile of v0, /device:TPU:2, one launch (start us, length us, event | category | flops | bytes accessed | tf_op | source)
XLA Modules:
  0.0 825.3 jit_solution(14754247701670380773)
XLA Ops:
  7.2 1.9 copy.29
  9.1 10.3 %all-to-all-start.1 = ((bf16[128,8,128]{0,2,1:T(8,128)(2,1)}), bf16[128,8,128]{0,2,1:T(8,128)(2,1)S(1)}, u32[]{:S(2)}, u32[]{:S(2)}) async-start(bf16[128,8,128]{0,2,1:T(8,128)(2,1)} %bitcast.3), calls=%async_computation.1 | async-start | bytes 524288 | tf_op jit(solution)/shard_map/all_to_all | solution.py:26
  19.4 1.8 copy.33
  21.1 11.0 %all-to-all-done.1 = bf16[128,8,128]{0,2,1:T(8,128)(2,1)S(1)} async-done(((bf16[128,8,128]{0,2,1:T(8,128)(2,1)}), bf16[128,8,128]{0,2,1:T(8,128)(2,1)S(1)}, u32[]{:S(2)}, u32[]{:S(2)}) %all-to-all-start.1) | async-done | bytes 262176 | tf_op jit(solution)/shard_map/all_to_all | solution.py:26
  32.1 3.4 all-to-all-start.3
  35.6 1.3 copy.27
  36.9 10.7 %all-to-all-done.3 = bf16[128,8,128]{0,2,1:T(8,128)(2,1)S(1)} async-done(((bf16[128,8,128]{0,2,1:T(8,128)(2,1)}), bf16[128,8,128]{0,2,1:T(8,128)(2,1)S(1)}, u32[]{:S(2)}, u32[]{:S(2)}) %all-to-all-start.3) | async-done | bytes 262176 | tf_op jit(solution)/shard_map/all_to_all | solution.py:27
  47.6 3.6 all-to-all-start
  51.1 1.4 copy.31
  52.5 28.0 %all-to-all-done = bf16[128,8,512]{0,2,1:T(8,128)(2,1)S(1)} async-done(((bf16[128,8,512]{0,2,1:T(8,128)(2,1)}), bf16[128,8,512]{0,2,1:T(8,128)(2,1)S(1)}, u32[]{:S(2)}, u32[]{:S(2)}) %all-to-all-start) | async-done | bytes 1048608 | tf_op jit(solution)/shard_map/all_to_all | solution.py:25
  80.5 3.6 all-to-all-start.2
  87.9 23.6 %all-to-all-done.2 = bf16[128,8,512]{0,2,1:T(8,128)(2,1)S(1)} async-done(((bf16[128,8,512]{0,2,1:T(8,128)(2,1)}), bf16[128,8,512]{0,2,1:T(8,128)(2,1)S(1)}, u32[]{:S(2)}, u32[]{:S(2)}) %all-to-all-start.2) | async-done | bytes 1048608 | tf_op jit(solution)/shard_map/all_to_all | solution.py:28
  121.6 1.8 fusion
  123.4 3.0 fusion.10
  126.4 2.2 multiply_reduce_fusion
  128.7 5.4 multiply_reduce_fusion.3
  138.3 1.8 fusion.44
  142.0 1.3 convolution_add_fusion.1
  143.3 17.0 %all-gather.2.cloned.1.call-done = bf16[1024,4096]{1,0:T(8,128)(2,1)} async-done(((bf16[128,4096]{1,0:T(8,128)(2,1)}), bf16[1024,4096]{1,0:T(8,128)(2,1)}) %all-gather.2.cloned.1.call-update) | async-done | bytes 8388624 | tf_op jit(solution)/shard_map/all_gather | solution.py:102
  160.3 7.2 convolution_bitcast_fusion
  167.5 6.1 convolution_bitcast_fusion.1
  179.2 24.3 %all-to-all-start.4 = ((bf16[8,128,512]{1,2,0:T(8,128)(2,1)}), bf16[8,128,512]{1,2,0:T(8,128)(2,1)S(1)}, u32[]{:S(2)}, u32[]{:S(2)}) async-start(bf16[8,128,512]{1,2,0:T(8,128)(2,1)} %copy_bitcast_fusion), calls=%async_computation.4 | async-start | bytes 2097152 | tf_op jit(solution)/shard_map/all_to_all | solution.py:100
  203.5 29.6 %all-to-all-done.4 = bf16[8,128,512]{1,2,0:T(8,128)(2,1)S(1)} async-done(((bf16[8,128,512]{1,2,0:T(8,128)(2,1)}), bf16[8,128,512]{1,2,0:T(8,128)(2,1)S(1)}, u32[]{:S(2)}, u32[]{:S(2)}) %all-to-all-start.4) | async-done | bytes 1048608 | tf_op jit(solution)/shard_map/all_to_all | solution.py:100
  234.4 580.8 %all-reduce.5.cloned.1.call-done = (f32[4096,128]{0,1:T(8,128)}, f32[4096,128]{0,1:T(8,128)}) async-done(((f32[4096,128]{0,1:T(8,128)}, f32[4096,128]{0,1:T(8,128)}), (f32[4096,128]{0,1:T(8,128)}, f32[4096,128]{0,1:T(8,128)})) %all-reduce.5.cloned.1.call-update) | async-done | bytes 4194320 | tf_op jit(solution)/shard_map/psum | solution.py:109
  (114 shorter events, 29.7 us)
Async XLA Ops:
  7.2 28.4 %copy-start.19 = (bf16[128,4096]{1,0:T(8,128)(2,1)S(1)}, bf16[128,4096]{1,0:T(8,128)(2,1)}, u32[]{:S(2)}) copy-start(bf16[128,4096]{1,0:T(8,128)(2,1)} %param.53) | copy-start | bytes 3145732
  9.1 23.1 %all-to-all-start.1 = ((bf16[128,8,128]{0,2,1:T(8,128)(2,1)}), bf16[128,8,128]{0,2,1:T(8,128)(2,1)S(1)}, u32[]{:S(2)}, u32[]{:S(2)}) async-start(bf16[128,8,128]{0,2,1:T(8,128)(2,1)} %bitcast.3), calls=%async_computation.1 | async-start | bytes 524288 | tf_op jit(solution)/shard_map/all_to_all | solution.py:26
  32.1 15.4 %all-to-all-start.3 = ((bf16[128,8,128]{0,2,1:T(8,128)(2,1)}), bf16[128,8,128]{0,2,1:T(8,128)(2,1)S(1)}, u32[]{:S(2)}, u32[]{:S(2)}) async-start(bf16[128,8,128]{0,2,1:T(8,128)(2,1)} %bitcast.9), calls=%async_computation.3 | async-start | bytes 524288 | tf_op jit(solution)/shard_map/all_to_all | solution.py:27
  35.5 15.6 %copy-start.20 = (bf16[128,4096]{1,0:T(8,128)(2,1)S(1)}, bf16[128,4096]{1,0:T(8,128)(2,1)}, u32[]{:S(2)}) copy-start(bf16[128,4096]{1,0:T(8,128)(2,1)} %param.56) | copy-start | bytes 3145732
  47.6 32.9 %all-to-all-start = ((bf16[128,8,512]{0,2,1:T(8,128)(2,1)}), bf16[128,8,512]{0,2,1:T(8,128)(2,1)S(1)}, u32[]{:S(2)}, u32[]{:S(2)}) async-start(bf16[128,8,512]{0,2,1:T(8,128)(2,1)} %bitcast), calls=%async_computation | async-start | bytes 2097152 | tf_op jit(solution)/shard_map/all_to_all | solution.py:25
  80.5 31.0 %all-to-all-start.2 = ((bf16[128,8,512]{0,2,1:T(8,128)(2,1)}), bf16[128,8,512]{0,2,1:T(8,128)(2,1)S(1)}, u32[]{:S(2)}, u32[]{:S(2)}) async-start(bf16[128,8,512]{0,2,1:T(8,128)(2,1)} %bitcast.6), calls=%async_computation.2 | async-start | bytes 2097152 | tf_op jit(solution)/shard_map/all_to_all | solution.py:28
  84.1 76.2 %all-gather.2.cloned.1.call-start = ((), (), s32[]{:S(2)}) async-start(), calls=%async_computation.5 | async-start | bytes 9437184 | tf_op jit(solution)/shard_map/all_gather | solution.py:102
  84.8 730.4 %all-reduce.5.cloned.1.call-start = ((), (), s32[]{:S(2)}) async-start(), calls=%async_computation.6 | async-start | bytes 8388608 | tf_op jit(solution)/shard_map/psum | solution.py:109
  87.9 33.7 %copy-start.4 = (bf16[8,128,512]{2,1,0:T(8,128)(2,1)}, bf16[8,128,512]{2,1,0:T(8,128)(2,1)S(1)}, u32[]{:S(2)}) copy-start(bf16[8,128,512]{2,1,0:T(8,128)(2,1)S(1)} %copy.28) | copy-start | bytes 3145732
  112.0 5.9 copy-start.16
  118.6 1.2 copy-start.8
  119.4 1.2 copy-start.17
  119.4 1.3 copy-start.18
  134.1 3.8 copy-start.14
  134.1 1.6 copy-start.5
  136.6 1.3 copy-start.2
  137.0 1.3 copy-start.22
  173.6 1.3 copy-start.13
  173.6 1.6 copy-start.11
  174.6 1.1 copy-start.7
  174.6 1.5 copy-start.15
  174.6 1.9 copy-start.3
  175.2 1.9 copy-start.1
  179.2 53.9 %all-to-all-start.4 = ((bf16[8,128,512]{1,2,0:T(8,128)(2,1)}), bf16[8,128,512]{1,2,0:T(8,128)(2,1)S(1)}, u32[]{:S(2)}, u32[]{:S(2)}) async-start(bf16[8,128,512]{1,2,0:T(8,128)(2,1)} %copy_bitcast_fusion), calls=%async_computation.4 | async-start | bytes 2097152 | tf_op jit(solution)/shard_map/all_to_all | solution.py:100
  (6 other events, 5.4 us)
Sparse Core Ops, SparseCore 0:
  87.0 73.1 all-gather.1
  173.7 641.4 all-reduce.4
where the time goes:
time: 826 us; the launch traced here: 825 us
  waiting for transfers between devices  701 us (85%)
  starting transfers between devices  45.2 us (5%)
  matrix products  36.6 us (4%)
  local copies, waits for them, and re-layouts  18.5 us (2%)
  between operations  14.6 us (2%)
  other arithmetic  9.06 us (1%)
    psum x1, waiting for transfers between devices, local(): key_full, value_full = lax.psum((key_part, value_part), 'dp')  581 us
    all_to_all x1, waiting for transfers between devices, local(): lax.all_to_all(head_query_grad, 'seq', split_axis=0, concat_axis=1, tiled...  29.6 us
    all_to_all x1, waiting for transfers between devices, local(): lax.all_to_all(queries, 'seq', split_axis=1, concat_axis=0, tiled=True)  28 us
    all_to_all x1, starting transfers between devices, local(): lax.all_to_all(head_query_grad, 'seq', split_axis=0, concat_axis=1, tiled...  24.3 us
    all_to_all x1, waiting for transfers between devices, local(): lax.all_to_all(out_grad, 'seq', split_axis=1, concat_axis=0, tiled=True)  23.6 us
    all_gather x1, waiting for transfers between devices, local(): piece = lax.all_gather(normed, 'seq', axis=0, tiled=True)  17 us
  transfers between devices with their start and end apart: 7, of which 7 were waited for; matrix products, arithmetic and copies ran while one was open for 5% of the time, Pallas kernels for 0%

commit v1 on v0

--- a/solution.py
+++ b/solution.py
@@ -99,7 +99,9 @@
     value_grad = value_acc.astype(jnp.bfloat16)
     query_grad = lax.all_to_all(head_query_grad, "seq", split_axis=0, concat_axis=1, tiled=True)
     width = normed.shape[1]
-    piece = lax.all_gather(normed, "seq", axis=0, tiled=True)
+    piece = jnp.concatenate(
+        lax.all_to_all(jnp.stack([normed] * lax.axis_size("seq")), "seq", 0, 0), axis=0
+    )
     key_part = lax.dot_general(
         piece, key_grad, (((0,), (0,)), ((), ())), preferred_element_type=jnp.float32
     )

time: 826 us -> 954 us (1.15)
  waiting for transfers between devices: 701 us -> 811 us
  blocking collectives: 0 us -> 31.6 us
  starting transfers between devices: 45.2 us -> 26.1 us
    all_to_all x1, waiting for transfers between devices: 23.6 us -> 151 us  [local(): lax.all_to_all(jnp.stack([normed] * lax.axis_size('seq')), 'seq', 0, 0)]
    all_to_all x0 -> x1, blocking collectives: none -> 31.6 us  [local(): lax.all_to_all(out_grad, 'seq', split_axis=1, concat_axis=0, tiled=True)]
    all_to_all x1, starting transfers between devices: 24.3 us -> 3.56 us  [local(): lax.all_to_all(head_query_grad, 'seq', split_axis=0, concat_axis=1, tiled...]
    all_gather x1 -> x0, waiting for transfers between devices: 17 us -> none  [local(): piece = lax.all_gather(normed, 'seq', axis=0, tiled=True)]
  transfers between devices with their start and end apart: 7 -> 6, of which waited for: 7 -> 6; matrix products, arithmetic and copies ran while one was open for 5% -> 4% of each run, Pallas kernels for 0% -> 0%
where the time goes in v1:
time: 954 us
  waiting for transfers between devices  811 us (85%)
  matrix products  36.5 us (4%)
  blocking collectives  31.6 us (3%)
  starting transfers between devices  26.1 us (3%)
  local copies, waits for them, and re-layouts  24.5 us (3%)
  between operations  14.6 us (2%)
    psum x1, waiting for transfers between devices, local(): key_full, value_full = lax.psum((key_part, value_part), 'dp')  582 us
    all_to_all x1, waiting for transfers between devices, local(): lax.all_to_all(jnp.stack([normed] * lax.axis_size('seq')), 'seq', 0, 0)  151 us
    all_to_all x1, blocking collectives, local(): lax.all_to_all(out_grad, 'seq', split_axis=1, concat_axis=0, tiled=True)  31.6 us
    all_to_all x1, waiting for transfers between devices, local(): lax.all_to_all(queries, 'seq', split_axis=1, concat_axis=0, tiled=True)  28.7 us
    all_to_all x1, waiting for transfers between devices, local(): lax.all_to_all(head_query_grad, 'seq', split_axis=0, concat_axis=1, tiled...  27.9 us
  transfers between devices with their start and end apart: 6, of which 6 were waited for; matrix products, arithmetic and copies ran while one was open for 4% of the time, Pallas kernels for 0%

profile of v1, /device:TPU:2, one launch (start us, length us, event | category | flops | bytes accessed | tf_op | source)
XLA Modules:
  0.0 953.5 jit_solution(18110908405676238644)
XLA Ops:
  7.2 1.9 copy.29
  9.1 10.3 %all-to-all-start.1 = ((bf16[128,8,128]{0,2,1:T(8,128)(2,1)}), bf16[128,8,128]{0,2,1:T(8,128)(2,1)S(1)}, u32[]{:S(2)}, u32[]{:S(2)}) async-start(bf16[128,8,128]{0,2,1:T(8,128)(2,1)} %bitcast.3), calls=%async_computation.1 | async-start | bytes 524288 | tf_op jit(solution)/shard_map/all_to_all | solution.py:26
  19.4 1.8 copy.33
  21.1 11.0 %all-to-all-done.1 = bf16[128,8,128]{0,2,1:T(8,128)(2,1)S(1)} async-done(((bf16[128,8,128]{0,2,1:T(8,128)(2,1)}), bf16[128,8,128]{0,2,1:T(8,128)(2,1)S(1)}, u32[]{:S(2)}, u32[]{:S(2)}) %all-to-all-start.1) | async-done | bytes 262176 | tf_op jit(solution)/shard_map/all_to_all | solution.py:26
  32.1 3.4 all-to-all-start.3
  35.6 1.3 copy.27
  36.9 10.7 %all-to-all-done.3 = bf16[128,8,128]{0,2,1:T(8,128)(2,1)S(1)} async-done(((bf16[128,8,128]{0,2,1:T(8,128)(2,1)}), bf16[128,8,128]{0,2,1:T(8,128)(2,1)S(1)}, u32[]{:S(2)}, u32[]{:S(2)}) %all-to-all-start.3) | async-done | bytes 262176 | tf_op jit(solution)/shard_map/all_to_all | solution.py:27
  48.3 3.6 all-to-all-start
  52.5 28.7 %all-to-all-done = bf16[128,8,512]{0,2,1:T(8,128)(2,1)S(1)} async-done(((bf16[128,8,512]{0,2,1:T(8,128)(2,1)}), bf16[128,8,512]{0,2,1:T(8,128)(2,1)S(1)}, u32[]{:S(2)}, u32[]{:S(2)}) %all-to-all-start) | async-done | bytes 1048608 | tf_op jit(solution)/shard_map/all_to_all | solution.py:25
  81.2 31.6 %all_to_all.100 = bf16[128,8,512]{0,2,1:T(8,128)(2,1)S(1)} all-to-all(bf16[128,8,512]{0,2,1:T(8,128)(2,1)S(1)} %bitcast.102), channel_id=1, replica_groups=mesh['dp'=64,'seq'=8] {'seq'}, dimensions={1} | all-to-all | bytes 2097152 | tf_op jit(solution)/shard_map/all_to_all | solution.py:28
  112.7 5.5 stack.5
  118.2 5.1 all-to-all-start.5
  137.2 1.8 fusion
  139.0 3.0 fusion.10
  142.1 2.2 multiply_reduce_fusion
  144.3 5.4 multiply_reduce_fusion.3
  153.9 1.8 fusion.51
  158.9 151.1 %all-to-all-done.5 = bf16[8,128,4096]{2,1,0:T(8,128)(2,1)} async-done(((bf16[8,128,4096]{2,1,0:T(8,128)(2,1)}), bf16[8,128,4096]{2,1,0:T(8,128)(2,1)}, u32[]{:S(2)}, u32[]{:S(2)}) %all-to-all-start.5) | async-done | bytes 8388640 | tf_op jit(solution)/shard_map/all_to_all | solution.py:103
  310.0 7.2 convolution_bitcast_fusion
  317.2 6.1 convolution_bitcast_fusion.1
  328.9 3.6 all-to-all-start.4
  332.5 27.9 %all-to-all-done.4 = bf16[8,128,512]{1,2,0:T(8,128)(2,1)S(1)} async-done(((bf16[8,128,512]{1,2,0:T(8,128)(2,1)}), bf16[8,128,512]{1,2,0:T(8,128)(2,1)S(1)}, u32[]{:S(2)}, u32[]{:S(2)}) %all-to-all-start.4) | async-done | bytes 1048608 | tf_op jit(solution)/shard_map/all_to_all | solution.py:100
  360.4 1.3 copy.38
  361.7 581.8 %all-reduce.5.cloned.1.call-done = (f32[4096,128]{0,1:T(8,128)}, f32[4096,128]{0,1:T(8,128)}) async-done(((f32[4096,128]{0,1:T(8,128)}, f32[4096,128]{0,1:T(8,128)}), (f32[4096,128]{0,1:T(8,128)}, f32[4096,128]{0,1:T(8,128)})) %all-reduce.5.cloned.1.call-update) | async-done | bytes 4194320 | tf_op jit(solution)/shard_map/psum | solution.py:111
  (121 shorter events, 31.0 us)
Async XLA Ops:
  7.2 28.4 %copy-start.21 = (bf16[128,4096]{1,0:T(8,128)(2,1)S(1)}, bf16[128,4096]{1,0:T(8,128)(2,1)}, u32[]{:S(2)}) copy-start(bf16[128,4096]{1,0:T(8,128)(2,1)} %param.53) | copy-start | bytes 3145732
  9.1 23.1 %all-to-all-start.1 = ((bf16[128,8,128]{0,2,1:T(8,128)(2,1)}), bf16[128,8,128]{0,2,1:T(8,128)(2,1)S(1)}, u32[]{:S(2)}, u32[]{:S(2)}) async-start(bf16[128,8,128]{0,2,1:T(8,128)(2,1)} %bitcast.3), calls=%async_computation.1 | async-start | bytes 524288 | tf_op jit(solution)/shard_map/all_to_all | solution.py:26
  32.1 15.4 %all-to-all-start.3 = ((bf16[128,8,128]{0,2,1:T(8,128)(2,1)}), bf16[128,8,128]{0,2,1:T(8,128)(2,1)S(1)}, u32[]{:S(2)}, u32[]{:S(2)}) async-start(bf16[128,8,128]{0,2,1:T(8,128)(2,1)} %bitcast.9), calls=%async_computation.3 | async-start | bytes 524288 | tf_op jit(solution)/shard_map/all_to_all | solution.py:27
  35.5 16.3 %copy-start.22 = (bf16[128,4096]{1,0:T(8,128)(2,1)S(1)}, bf16[128,4096]{1,0:T(8,128)(2,1)}, u32[]{:S(2)}) copy-start(bf16[128,4096]{1,0:T(8,128)(2,1)} %param.56) | copy-start | bytes 3145732
  48.3 32.9 %all-to-all-start = ((bf16[128,8,512]{0,2,1:T(8,128)(2,1)}), bf16[128,8,512]{0,2,1:T(8,128)(2,1)S(1)}, u32[]{:S(2)}, u32[]{:S(2)}) async-start(bf16[128,8,512]{0,2,1:T(8,128)(2,1)} %bitcast), calls=%async_computation | async-start | bytes 2097152 | tf_op jit(solution)/shard_map/all_to_all | solution.py:25
  118.2 6.1 copy-start.20
  118.2 191.8 %all-to-all-start.5 = ((bf16[8,128,4096]{2,1,0:T(8,128)(2,1)}), bf16[8,128,4096]{2,1,0:T(8,128)(2,1)}, u32[]{:S(2)}, u32[]{:S(2)}) async-start(bf16[8,128,4096]{2,1,0:T(8,128)(2,1)} %stack.5), calls=%async_computation.5 | async-start | bytes 16777216 | tf_op jit(solution)/shard_map/all_to_all | solution.py:103
  123.3 820.1 %all-reduce.5.cloned.1.call-start = ((), (), s32[]{:S(2)}) async-start(), calls=%async_computation.6 | async-start | bytes 8388608 | tf_op jit(solution)/shard_map/psum | solution.py:111
  126.6 10.6 %copy-start.4 = (bf16[8,128,512]{2,1,0:T(8,128)(2,1)}, bf16[8,128,512]{2,1,0:T(8,128)(2,1)S(1)}, u32[]{:S(2)}) copy-start(bf16[8,128,512]{2,1,0:T(8,128)(2,1)S(1)} %copy.28) | copy-start | bytes 3145732
  127.2 5.9 copy-start.16
  135.1 1.2 copy-start.17
  135.1 1.3 copy-start.18
  149.7 3.9 copy-start.14
  149.7 1.6 copy-start.5
  152.2 1.3 copy-start.2
  152.6 1.3 copy-start.26
  152.6 3.2 copy-start.24
  323.3 1.3 copy-start.13
  323.3 1.6 copy-start.11
  324.4 1.1 copy-start.7
  324.4 1.9 copy-start.3
  324.9 1.8 copy-start.15
  325.8 1.5 copy-start.1
  328.9 31.4 %all-to-all-start.4 = ((bf16[8,128,512]{1,2,0:T(8,128)(2,1)}), bf16[8,128,512]{1,2,0:T(8,128)(2,1)S(1)}, u32[]{:S(2)}, u32[]{:S(2)}) async-start(bf16[8,128,512]{1,2,0:T(8,128)(2,1)} %copy_bitcast_fusion), calls=%async_computation.4 | async-start | bytes 2097152 | tf_op jit(solution)/shard_map/all_to_all | solution.py:100
  (9 other events, 7.8 us)
Sparse Core Ops, SparseCore 0:
  323.5 619.9 all-reduce.4
